TPU v7x, 128 devices: a whole 4x4x4 slice. The times are simulated.
128 devices in a mesh: brick: 8 (over y, core), grp: 16 (over x, z).
Axes of the slice: x: 4, y: 4, z: 4, core: 2. Of those that a mesh axis runs over, the one named last changes fastest.
Arguments:
- source: float32 [16, 8, 2, 32, 1024], P('grp', 'brick'), may hold values from -21 to 21
- uptake: float32 [16, 8, 2, 32, 1024], P('grp', 'brick'), may hold values from 0.00015 to 0.006
- conductance: float32 [16, 8, 6, 2, 32, 1024], P('grp', 'brick'), may hold values from 0 to 3, as said below
- occupancy: int32 [16, 2, 8], replicated, may hold values from 0 to 1, as said below
- assignment: int32 [8], replicated, may hold values from 0 to 7, as said below
Outputs:
- solution_field: float32 [16, 8, 2, 32, 1024], P('grp', 'brick')
- residual: float32 [16, 8, 2, 32, 1024], P('grp', 'brick')
Inputs may be any that keep to these rules, and one draw needn't show every extreme that they name: `occupancy`: 1 marks an occupied brick; in every draw one patch of some slab has all its bricks occupied. `assignment`: each patch is held by exactly one index of brick. `conductance`: equal at both ends of a bond: the value toward +x at a cell is the value toward -x at its +x neighbour, likewise for y and z, the lattice being read cyclically; values toward +z and -z are 0.3 or more.
All inputs are finite; a program needn't handle non-finite values.
Results may differ from a plain program's by a relative error of at most 0.0003.
Values sent between devices are 32-bit elements; how exact they have to be, the bound alone decides.
A program may use at most 128 MiB of HBM per device.

v0:
```python
import jax
import jax.numpy as jnp
from jax import lax
from jax.sharding import PartitionSpec as P

BS = 32
PATCH_X = 1
PATCH_Y = 2
ITERS = 3
OMEGA = 0.6


def extended_2(block, sides, width):
    for axis, dim in sides:
        count = lax.axis_size(axis)
        forward = [(i, i + 1) for i in range(count - 1)]
        backward = [(target, source) for source, target in forward]
        low = lax.ppermute(
            lax.slice_in_dim(block, block.shape[dim] - width, None, axis=dim), axis, forward
        )
        high = lax.ppermute(lax.slice_in_dim(block, 0, width, axis=dim), axis, backward)
        block = jnp.concatenate([low, block, high], axis=dim)
    return block


def assemble(coarse_diag, couplings, strides):
    extent = coarse_diag.shape[0]
    matrix = jnp.diag(coarse_diag)
    for coupling, stride in zip(couplings, strides):
        banded = coupling[: extent - stride]
        matrix = matrix - jnp.diag(banded, stride) - jnp.diag(banded, -stride)
    return matrix


def pad_rows(block, capacity):
    return jnp.pad(block, ((0, capacity - block.shape[0]), (0, 0)))


def on_device(source, uptake, conductance, occupancy, assignment):
    face_size = BS * BS
    capacity = max(PATCH_X, PATCH_Y)
    slot_count = PATCH_X * PATCH_Y
    slab_index = lax.axis_index("grp")
    brick_index = lax.axis_index("brick")
    brick_count = lax.axis_size("brick")
    across = brick_count // 2
    peer_ids = jnp.arange(brick_count, dtype=jnp.int32)
    patch_index = assignment[brick_index]
    patch_row = patch_index // across
    patch_column = patch_index % across

    def owner_of(row_shift, column_shift):
        row_target = patch_row + row_shift
        column_target = patch_column + column_shift
        inside = (
            (row_target >= 0) & (row_target < 2) & (column_target >= 0) & (column_target < across)
        )
        holder = jnp.sum(jnp.where(assignment == row_target * across + column_target, peer_ids, 0))
        return jnp.where(inside, holder, -1)

    wanted = jnp.stack([owner_of(1, 0), owner_of(-1, 0), owner_of(0, 1), owner_of(0, -1)])
    padded = jnp.pad(occupancy, 1)
    window = lax.dynamic_slice(
        padded,
        (slab_index, patch_row * PATCH_X, patch_column * PATCH_Y),
        (3, PATCH_X + 2, PATCH_Y + 2),
    ).astype(jnp.float32)
    centre = window[1, 1:-1, 1:-1].reshape(slot_count)
    toward = [
        window[1, 2:, 1:-1],
        window[1, :-2, 1:-1],
        window[1, 1:-1, 2:],
        window[1, 1:-1, :-2],
        window[2, 1:-1, 1:-1],
        window[0, 1:-1, 1:-1],
    ]
    first_axis = lax.broadcasted_iota(jnp.int32, (1, BS, face_size), 1)
    flat_axis = lax.broadcasted_iota(jnp.int32, (1, BS, face_size), 2)
    second_axis = flat_axis // BS
    third_axis = flat_axis % BS
    cube_third = lax.broadcasted_iota(jnp.int32, (1, BS, BS, BS), 3)
    borders = [
        first_axis == BS - 1,
        first_axis == 0,
        second_axis == BS - 1,
        second_axis == 0,
        third_axis == BS - 1,
        third_axis == 0,
    ]
    bonds = conductance[0, 0]
    live_here = centre[:, None, None]
    effective = []
    for direction in range(6):
        neighbour_live = toward[direction].reshape(slot_count)[:, None, None]
        active = jnp.where(borders[direction], live_here * neighbour_live, live_here)
        effective.append(bonds[direction] * active)
    absorb = uptake[0, 0]
    diagonal = absorb
    for direction in range(6):
        diagonal = diagonal + effective[direction]

    def apply_operator(field):
        lower_x = field[:, 0, :]
        upper_x = field[:, BS - 1, :]
        lower_y = field[:, :, :BS].reshape(slot_count, face_size)
        upper_y = field[:, :, face_size - BS :].reshape(slot_count, face_size)
        cube = field.reshape(slot_count, BS, BS, BS)
        lower_z = cube[:, :, :, 0].reshape(slot_count, face_size)
        upper_z = cube[:, :, :, BS - 1].reshape(slot_count, face_size)
        grid_lower_x = lower_x.reshape(PATCH_X, PATCH_Y, face_size)
        grid_upper_x = upper_x.reshape(PATCH_X, PATCH_Y, face_size)
        grid_lower_y = lower_y.reshape(PATCH_X, PATCH_Y, face_size)
        grid_upper_y = upper_y.reshape(PATCH_X, PATCH_Y, face_size)
        outgoing_sides = jnp.stack(
            [
                pad_rows(grid_lower_x[0], capacity),
                pad_rows(grid_upper_x[PATCH_X - 1], capacity),
                pad_rows(grid_lower_y[:, 0], capacity),
                pad_rows(grid_upper_y[:, PATCH_Y - 1], capacity),
            ]
        )
        portion = lax.all_gather(outgoing_sides[None], "brick", axis=0, tiled=True)
        sources = jnp.arange(portion.shape[0], dtype=jnp.int32)
        matches = sources[:, None] == wanted[None, :]
        remote = jnp.zeros((4, capacity, face_size), jnp.float32) + jnp.sum(
            jnp.where(matches[:, :, None, None], portion, 0.0), axis=0
        )
        stacked = jnp.stack([lower_z, upper_z])
        extended = extended_2(stacked, (("grp", 0),), 1)
        from_below = extended[0].reshape(slot_count, BS, BS, 1)
        from_above = extended[3].reshape(slot_count, BS, BS, 1)
        beyond_xplus = jnp.concatenate(
            [grid_lower_x[1:], remote[0, :PATCH_Y][None]], axis=0
        ).reshape(slot_count, face_size)
        beyond_xminus = jnp.concatenate(
            [remote[1, :PATCH_Y][None], grid_upper_x[:-1]], axis=0
        ).reshape(slot_count, face_size)
        beyond_yplus = jnp.concatenate(
            [grid_lower_y[:, 1:], remote[2, :PATCH_X][:, None]], axis=1
        ).reshape(slot_count, BS, BS)
        beyond_yminus = jnp.concatenate(
            [remote[3, :PATCH_X][:, None], grid_upper_y[:, :-1]], axis=1
        ).reshape(slot_count, BS, BS)
        upper_neighbour = jnp.where(
            cube_third == BS - 1, from_above, jnp.roll(cube, -1, axis=3)
        ).reshape(slot_count, BS, face_size)
        lower_neighbour = jnp.where(cube_third == 0, from_below, jnp.roll(cube, 1, axis=3)).reshape(
            slot_count, BS, face_size
        )
        total = diagonal * field
        total = total - effective[0] * jnp.concatenate(
            [field[:, 1:, :], beyond_xplus[:, None, :]], axis=1
        )
        total = total - effective[1] * jnp.concatenate(
            [beyond_xminus[:, None, :], field[:, :-1, :]], axis=1
        )
        total = total - effective[2] * jnp.concatenate([field[:, :, BS:], beyond_yplus], axis=2)
        total = total - effective[3] * jnp.concatenate(
            [beyond_yminus, field[:, :, : face_size - BS]], axis=2
        )
        total = total - effective[4] * upper_neighbour
        total = total - effective[5] * lower_neighbour
        return total

    slot_ids = jnp.arange(slot_count)
    brick_first = slot_ids // PATCH_Y
    brick_second = slot_ids % PATCH_Y
    inside = [
        (brick_first < PATCH_X - 1).astype(jnp.float32),
        (brick_first > 0).astype(jnp.float32),
        (brick_second < PATCH_Y - 1).astype(jnp.float32),
        (brick_second > 0).astype(jnp.float32),
    ]
    face_sums = [
        jnp.sum(effective[0][:, BS - 1, :], axis=1),
        jnp.sum(effective[1][:, 0, :], axis=1),
        jnp.sum(effective[2][:, :, face_size - BS :], axis=(1, 2)),
        jnp.sum(effective[3][:, :, :BS], axis=(1, 2)),
        jnp.sum(effective[4].reshape(slot_count, BS, BS, BS)[:, :, :, BS - 1], axis=(1, 2)),
        jnp.sum(effective[5].reshape(slot_count, BS, BS, BS)[:, :, :, 0], axis=(1, 2)),
    ]
    coarse_diag = jnp.sum(absorb, axis=(1, 2))
    for direction in range(4):
        coarse_diag = coarse_diag + face_sums[direction] * inside[direction]
    coarse_diag = coarse_diag + face_sums[4] + face_sums[5]
    record = jnp.stack(
        [coarse_diag, face_sums[0] * inside[0], face_sums[2] * inside[2], face_sums[4]]
    )[None]
    gathered = lax.all_gather(record, "grp", axis=0, tiled=True)
    columns = jnp.transpose(gathered, (1, 0, 2)).reshape(4, -1)
    matrix = assemble(columns[0], (columns[1], columns[2], columns[3]), (PATCH_Y, 1, slot_count))
    factor = jnp.linalg.cholesky(matrix)

    def coarse_solve(residual_field):
        totals = jnp.sum(residual_field, axis=(1, 2))
        gathered_terms = lax.all_gather(totals[None], "grp", axis=0, tiled=True).reshape(-1, 1)
        middle = lax.linalg.triangular_solve(factor, gathered_terms, left_side=True, lower=True)
        result = lax.linalg.triangular_solve(
            factor, middle, left_side=True, lower=True, transpose_a=True
        )
        return lax.dynamic_slice_in_dim(result[:, 0], slab_index * slot_count, slot_count)

    def precondition(residual_field):
        smoothed = OMEGA * residual_field / diagonal
        smoothed = smoothed + OMEGA * (residual_field - apply_operator(smoothed)) / diagonal
        return smoothed + coarse_solve(residual_field)[:, None, None]

    forcing = source[0, 0] * live_here
    solution_field = jnp.zeros_like(forcing)
    residual = forcing

    def global_sum(values):
        return lax.psum(jnp.sum(values), ("brick", "grp"))

    search = precondition(residual)
    energy = global_sum(residual * search)
    for iteration in range(ITERS):
        mapped = apply_operator(search)
        step_size = energy / global_sum(search * mapped)
        solution_field = solution_field + step_size * search
        residual = residual - step_size * mapped
        if iteration + 1 < ITERS:
            smoothed = precondition(residual)
            renewed = global_sum(residual * smoothed)
            search = smoothed + renewed / energy * search
            energy = renewed
    return (solution_field[None, None], residual[None, None])


def solution(mesh):
    return jax.shard_map(
        on_device,
        mesh=mesh,
        in_specs=(
            P("grp", "brick", None, None, None),
            P("grp", "brick", None, None, None),
            P("grp", "brick", None, None, None, None),
            P(),
            P(),
        ),
        out_specs=(P("grp", "brick", None, None, None), P("grp", "brick", None, None, None)),
        check_vma=False,
    )
```

profile of v0, /device:TPU:1, one launch (start us, length us, event | category | flops | bytes accessed | tf_op | source)
XLA Modules:
  0.0 1063.9 jit_solution(14409875242148923339)
XLA Ops:
  15.4 2.4 squeeze.120
  22.2 5.7 multiply_divide_fusion.2
  30.5 4.9 collective-permute-start.1
  45.7 14.1 %all-gather = f32[32,2,1024]{2,1,0:T(2,128)S(1)} all-gather(f32[4,2,1024]{2,1,0:T(2,128)S(1)} %copy.294), channel_id=2, replica_groups=mesh['brick'=8,'grp'=16] {'brick'}, dimensions={0}, use_global_device_ids=true | all-gather | bytes 294912 | tf_op jit(solution)/shard_map/all_gather | solution.py:122
  68.6 19.9 %all-gather.10 = f32[16,4,2]{1,2,0:T(2,128)S(1)} all-gather(f32[1,4,2]{1,2,0:T(2,128)S(1)} %bitcast.616), channel_id=3, replica_groups=mesh['brick'=8,'grp'=16] {'grp'}, dimensions={0}, use_global_device_ids=true | all-gather | bytes 544 | tf_op jit(solution)/shard_map/all_gather | solution.py:189
  94.2 31.1 %all-reduce.18 = f32[32]{0:T(128)S(1)} all-reduce(f32[32]{0:T(128)S(1)} %dynamic-update-slice.3), channel_id=4, replica_groups=mesh['brick'=8,'grp'=16] {'grp'}, use_global_device_ids=true, to_apply=%add.18 | all-reduce | flops 32 | bytes 256 | tf_op jit(solution)/shard_map/triangular_solve/reshape.87 | solution.py:197
  130.3 2.9 cholesky.19
  134.6 2.4 custom-call.14
  153.2 8.4 fusion.46
  161.6 2.4 concatenate.643
  164.0 2.4 concatenate.645
  167.8 2.4 broadcast_in_dim.696
  171.5 2.4 broadcast_in_dim.702
  184.6 25.6 %all-gather.3 = f32[32,2,1024]{2,1,0:T(2,128)S(1)} all-gather(f32[4,2,1024]{2,1,0:T(2,128)S(1)} %copy.298), channel_id=5, replica_groups=mesh['brick'=8,'grp'=16] {'brick'}, dimensions={0}, use_global_device_ids=true | all-gather | bytes 294912 | tf_op jit(solution)/shard_map/all_gather | solution.py:122
  226.1 3.0 pad_maximum_fusion.2
  231.1 2.4 concatenate.676
  233.6 2.4 concatenate.677
  236.0 2.4 broadcast_in_dim.743
  251.7 2.4 concatenate.726
  258.9 2.4 concatenate.663
  271.8 2.4 broadcast_in_dim.729
  277.7 2.4 broadcast_in_dim.761
  280.1 2.4 broadcast_in_dim.726
  282.5 3.7 multiply_reduce_fusion.3
  286.2 64.0 %all-reduce.21 = (f32[]{:T(128)}, f32[]{:T(128)}) all-reduce(f32[]{:T(128)} %get-tuple-element.21, f32[]{:T(128)} %get-tuple-element.20), channel_id=1, replica_groups=mesh['brick'=8,'grp'=16] {'brick','grp'}, use_global_device_ids=true, to_apply=%region_16.19 | all-reduce | flops 2 | bytes 16 | tf_op jit(solution)/shard_map/psum | solution.py:213
  362.0 13.5 %all-gather.4 = f32[32,2,1024]{2,1,0:T(2,128)S(1)} all-gather(f32[4,2,1024]{2,1,0:T(2,128)S(1)} %copy.304), channel_id=6, replica_groups=mesh['brick'=8,'grp'=16] {'brick'}, dimensions={0}, use_global_device_ids=true | all-gather | bytes 294912 | tf_op jit(solution)/shard_map/all_gather | solution.py:122
  385.3 9.1 multiply_divide_fusion.1
  400.2 31.6 %all-reduce.19 = f32[32]{0:T(128)} all-reduce(f32[32]{0:T(128)} %dynamic-update-slice.4), channel_id=7, replica_groups=mesh['brick'=8,'grp'=16] {'grp'}, use_global_device_ids=true, to_apply=%add.19 | all-reduce | flops 32 | bytes 256 | tf_op jit(solution)/shard_map/triangular_solve/reshape.87 | solution.py:197
  442.0 3.0 pad_maximum_fusion.4
  447.3 3.0 fusion.96
  478.9 2.4 broadcast_in_dim.752
  487.2 3.7 multiply_reduce_fusion.2
  490.9 71.1 %psum.44 = f32[]{:T(128)} all-reduce(f32[]{:T(128)} %get-tuple-element.54), channel_id=1, replica_groups=mesh['brick'=8,'grp'=16] {'brick','grp'}, use_global_device_ids=true, to_apply=%region_23.26 | all-reduce | flops 1 | bytes 8 | tf_op jit(solution)/shard_map/psum | solution.py:213
  565.9 13.6 %all-gather.6 = f32[32,2,1024]{2,1,0:T(2,128)S(1)} all-gather(f32[4,2,1024]{2,1,0:T(2,128)S(1)} %copy.309), channel_id=8, replica_groups=mesh['brick'=8,'grp'=16] {'brick'}, dimensions={0}, use_global_device_ids=true | all-gather | bytes 294912 | tf_op jit(solution)/shard_map/all_gather | solution.py:122
  588.0 7.3 multiply_add_fusion.1
  603.4 2.7 pad_maximum_fusion.6
  607.5 2.5 broadcast_in_dim.764
  610.0 2.4 broadcast_in_dim.763
  620.1 2.5 concatenate.791
  630.3 2.5 broadcast_in_dim.760
  637.4 3.3 multiply_reduce_fusion.1
  640.7 66.1 %psum.45 = f32[]{:T(128)} all-reduce(f32[]{:T(128)} %get-tuple-element.50), channel_id=1, replica_groups=mesh['brick'=8,'grp'=16] {'brick','grp'}, use_global_device_ids=true, to_apply=%region_26.29 | all-reduce | flops 1 | bytes 8 | tf_op jit(solution)/shard_map/psum | solution.py:213
  711.4 13.5 %all-gather.7 = f32[32,2,1024]{2,1,0:T(2,128)S(1)} all-gather(f32[4,2,1024]{2,1,0:T(2,128)S(1)} %copy.314), channel_id=9, replica_groups=mesh['brick'=8,'grp'=16] {'brick'}, dimensions={0}, use_global_device_ids=true | all-gather | bytes 294912 | tf_op jit(solution)/shard_map/all_gather | solution.py:122
  733.8 8.2 multiply_divide_fusion
  747.8 31.5 %all-reduce.20 = f32[32]{0:T(128)} all-reduce(f32[32]{0:T(128)} %dynamic-update-slice.5), channel_id=10, replica_groups=mesh['brick'=8,'grp'=16] {'grp'}, use_global_device_ids=true, to_apply=%add.20 | all-reduce | flops 32 | bytes 256 | tf_op jit(solution)/shard_map/triangular_solve/reshape.87 | solution.py:197
  788.1 3.0 pad_maximum_fusion.8
  793.0 2.4 broadcast_in_dim.781
  805.9 2.4 concatenate.804
  810.8 2.4 concatenate.805
  813.2 2.4 concatenate.759
  823.6 2.4 broadcast_in_dim.771
  829.5 2.4 broadcast_in_dim.768
  831.9 3.8 multiply_reduce_fusion
  835.8 70.9 %psum.46 = f32[]{:T(128)} all-reduce(f32[]{:T(128)} %get-tuple-element.42), channel_id=1, replica_groups=mesh['brick'=8,'grp'=16] {'brick','grp'}, use_global_device_ids=true, to_apply=%region_30.33 | all-reduce | flops 1 | bytes 8 | tf_op jit(solution)/shard_map/psum | solution.py:213
  914.6 13.8 %all-gather.9 = f32[32,2,1024]{2,1,0:T(2,128)S(1)} all-gather(f32[4,2,1024]{2,1,0:T(2,128)S(1)} %copy.319), channel_id=11, replica_groups=mesh['brick'=8,'grp'=16] {'brick'}, dimensions={0}, use_global_device_ids=true | all-gather | bytes 294912 | tf_op jit(solution)/shard_map/all_gather | solution.py:122
  938.2 10.7 %multiply_add_fusion = f32[2,32,32,32]{3,2,1,0:T(8,128)S(1)} fusion(f32[2,32,32,32]{3,2,1,0:T(8,128)} %copy-done.5, f32[2,32,32,32]{3,2,1,0:T(8,128)} %get-tuple-element.75, f32[2,32,32,32]{3,2,1,0:T(8,128)} %get-tuple-element.77, f32[2,32,32,32]{3,2,1,0:T(8,128)} %get-tuple-element.76, f32[2,32,32,32]{3,2,1,0:T(8,128)} %concatenate.773, ...), kind=kLoop, calls=%fused_computation.76 | loop fusion | flops 3735552 | bytes 5865592 | tf_op jit(solution)/shard_map/add | solution.py:225
  959.3 2.4 broadcast_in_dim.783
  961.7 2.4 broadcast_in_dim.782
  966.9 2.4 concatenate.818
  969.3 2.4 concatenate.775
  978.0 2.5 broadcast_in_dim.779
  984.3 2.6 fusion.155
  988.6 66.6 %psum.47 = f32[]{:T(128)} all-reduce(f32[]{:T(128)} %fusion.155), channel_id=1, replica_groups=mesh['brick'=8,'grp'=16] {'brick','grp'}, use_global_device_ids=true, to_apply=%region_33.36 | all-reduce | flops 1 | bytes 8 | tf_op jit(solution)/shard_map/psum | solution.py:213
  1056.6 6.0 fusion.149
  (697 shorter events, 333.0 us)
Async XLA Ops:
  0.6 9.8 copy-start.37
  0.6 11.2 %copy-start = (f32[1,1,6,2,32,1024]{5,4,3,2,1,0:T(8,128)S(1)}, f32[1,1,6,2,32,1024]{5,4,3,2,1,0:T(8,128)}, u32[]{:S(2)}) copy-start(f32[1,1,6,2,32,1024]{5,4,3,2,1,0:T(8,128)} %param.11) | copy-start | bytes 4718596
  4.7 34.9 %copy-start.95 = (pred[32]{0:T(512)(128)(4,1)}, pred[32]{0:T(512)(128)(4,1)S(1)}, u32[]{:S(2)}) copy-start(pred[32]{0:T(512)(128)(4,1)S(1)} %get-tuple-element.277) | copy-start | bytes 100
  4.7 34.9 %copy-start.101 = (pred[32]{0:T(512)(128)(4,1)}, pred[32]{0:T(512)(128)(4,1)S(1)}, u32[]{:S(2)}) copy-start(pred[32]{0:T(512)(128)(4,1)S(1)} %get-tuple-element.278) | copy-start | bytes 100
  8.2 31.4 %copy-start.85 = (f32[2]{0:T(128)}, f32[2]{0:T(128)S(1)}, u32[]{:S(2)}) copy-start(f32[2]{0:T(128)S(1)} %get-tuple-element.32) | copy-start | bytes 28
  15.3 6.9 copy-start.1
  22.2 17.4 %copy-start.118 = (f32[2]{0:T(128)}, f32[2]{0:T(128)S(1)}, u32[]{:S(2)}) copy-start(f32[2]{0:T(128)S(1)} %get-tuple-element.268) | copy-start | bytes 28
  27.9 10.7 %copy-start.20 = (f32[1,1,2,32,1024]{4,3,2,1,0:T(8,128)S(1)}, f32[1,1,2,32,1024]{4,3,2,1,0:T(8,128)}, u32[]{:S(2)}) copy-start(f32[1,1,2,32,1024]{4,3,2,1,0:T(8,128)} %param.9) | copy-start | bytes 786436
  28.0 11.6 %copy-start.38 = (f32[1,1,2,32,1024]{4,3,2,1,0:T(8,128)S(1)}, f32[1,1,2,32,1024]{4,3,2,1,0:T(8,128)}, u32[]{:S(2)}) copy-start(f32[1,1,2,32,1024]{4,3,2,1,0:T(8,128)} %param.10) | copy-start | bytes 786436
  28.0 11.6 %copy-start.122 = (f32[2]{0:T(128)S(1)}, f32[2]{0:T(128)}, u32[]{:S(2)}) copy-start(f32[2]{0:T(128)} %copy-done.121) | copy-start | bytes 28
  28.0 11.6 %copy-start.125 = (f32[2]{0:T(128)S(1)}, f32[2]{0:T(128)}, u32[]{:S(2)}) copy-start(f32[2]{0:T(128)} %copy-done.124) | copy-start | bytes 28
  28.0 11.6 %copy-start.130 = (f32[2]{0:T(128)S(1)}, f32[2]{0:T(128)}, u32[]{:S(2)}) copy-start(f32[2]{0:T(128)} %copy-done.129) | copy-start | bytes 28
  28.0 11.6 %copy-start.134 = (f32[2]{0:T(128)S(1)}, f32[2]{0:T(128)}, u32[]{:S(2)}) copy-start(f32[2]{0:T(128)} %copy-done.133) | copy-start | bytes 28
  28.0 11.6 %copy-start.138 = (f32[2]{0:T(128)S(1)}, f32[2]{0:T(128)}, u32[]{:S(2)}) copy-start(f32[2]{0:T(128)} %copy-done.137) | copy-start | bytes 28
  30.5 121.8 %collective-permute-start.1 = (f32[1,2,1024]{2,1,0:T(2,128)}, f32[1,2,1024]{2,1,0:T(2,128)}, u32[]{:S(2)}, u32[]{:S(2)}) collective-permute-start(f32[1,2,1024]{2,1,0:T(2,128)} %stack_reshape_squeeze.37), channel_id=1, source_target_pairs={{0,1},{1,2},{2,3},{3,4},{4,5},{5,6},{6,7},{7,8},{8,9},{9,10},{10,1... | collective-permute-start | bytes 24584 | tf_op jit(solution)/shard_map/ppermute | solution.py:18
  36.1 115.4 %collective-permute-start = (f32[1,2,1024]{2,1,0:T(2,128)}, f32[1,2,1024]{2,1,0:T(2,128)}, u32[]{:S(2)}, u32[]{:S(2)}) collective-permute-start(f32[1,2,1024]{2,1,0:T(2,128)} %stack_reshape_squeeze.36), channel_id=1, source_target_pairs={{1,0},{2,1},{3,2},{4,3},{5,4},{6,5},{7,6},{8,7},{9,8},{10,9},{11,1... | collective-permute-start | bytes 24584 | tf_op jit(solution)/shard_map/ppermute | solution.py:21
  40.7 19.9 %copy-start.31 = (f32[2,32,1024]{2,1,0:T(8,128)}, f32[2,32,1024]{2,1,0:T(8,128)S(1)}, u32[]{:S(2)}) copy-start(f32[2,32,1024]{2,1,0:T(8,128)S(1)} %get-tuple-element.68) | copy-start | bytes 786436
  40.7 27.0 %copy-start.13 = (f32[2,32,1024]{2,1,0:T(8,128)}, f32[2,32,1024]{2,1,0:T(8,128)S(1)}, u32[]{:S(2)}) copy-start(f32[2,32,1024]{2,1,0:T(8,128)S(1)} %get-tuple-element.73) | copy-start | bytes 786436
  40.7 446.4 %copy-start.11 = (f32[2,32,1024]{2,1,0:T(8,128)}, f32[2,32,1024]{2,1,0:T(8,128)S(1)}, u32[]{:S(2)}) copy-start(f32[2,32,1024]{2,1,0:T(8,128)S(1)} %get-tuple-element.72) | copy-start | bytes 786436
  44.2 16.4 %copy-start.141 = (pred[8,4]{1,0:T(8,128)(4,1)}, pred[8,4]{1,0:T(8,128)(4,1)S(1)}, u32[]{:S(2)}) copy-start(pred[8,4]{1,0:T(8,128)(4,1)S(1)} %iota_compare_fusion.11) | copy-start | bytes 100
  61.3 6.6 copy-start.3
  68.2 21.3 %copy-start.7 = (f32[2,32,32,32]{3,2,1,0:T(8,128)S(1)}, f32[2,32,32,32]{3,2,1,0:T(8,128)}, u32[]{:S(2)}) copy-start(f32[2,32,32,32]{3,2,1,0:T(8,128)} %copy-done.6) | copy-start | bytes 786436
  89.5 47.8 %copy-start.59 = (f32[2,32,992]{2,1,0:T(8,128)S(1)}, f32[2,32,992]{2,1,0:T(8,128)}, u32[]{:S(2)}) copy-start(f32[2,32,992]{2,1,0:T(8,128)} %get-tuple-element.146) | copy-start | bytes 761860
  91.3 53.5 %copy-start.96 = (pred[32]{0:T(512)(128)(4,1)S(1)}, pred[32]{0:T(512)(128)(4,1)}, u32[]{:S(2)}) copy-start(pred[32]{0:T(512)(128)(4,1)} %copy-done.95) | copy-start | bytes 100
  91.3 54.2 %copy-start.102 = (pred[32]{0:T(512)(128)(4,1)S(1)}, pred[32]{0:T(512)(128)(4,1)}, u32[]{:S(2)}) copy-start(pred[32]{0:T(512)(128)(4,1)} %copy-done.101) | copy-start | bytes 100
  126.0 22.8 %copy-start.81 = (f32[2,32,32]{2,1,0:T(8,128)}, f32[2,32,32]{2,1,0:T(8,128)S(1)}, u32[]{:S(2)}) copy-start(f32[2,32,32]{2,1,0:T(8,128)S(1)} %reshape.2206) | copy-start | bytes 24580
  126.8 22.1 %copy-start.82 = (f32[2,32,32]{2,1,0:T(8,128)}, f32[2,32,32]{2,1,0:T(8,128)S(1)}, u32[]{:S(2)}) copy-start(f32[2,32,32]{2,1,0:T(8,128)S(1)} %reshape.2205) | copy-start | bytes 24580
  137.4 11.5 %copy-start.57 = (f32[2,31,1024]{2,1,0:T(8,128)S(1)}, f32[2,31,1024]{2,1,0:T(8,128)}, u32[]{:S(2)}) copy-start(f32[2,31,1024]{2,1,0:T(8,128)} %get-tuple-element.142) | copy-start | bytes 761860
  138.6 14.4 %copy-start.156 = (f32[2]{0:T(128)}, f32[2]{0:T(128)S(1)}, u32[]{:S(2)}) copy-start(f32[2]{0:T(128)S(1)} %fusion.180) | copy-start | bytes 28
  221.3 44.6 %collective-permute-start.3 = (f32[1,2,1024]{2,1,0:T(2,128)}, f32[1,2,1024]{2,1,0:T(2,128)}, u32[]{:S(2)}, u32[]{:S(2)}) collective-permute-start(f32[1,2,1024]{2,1,0:T(2,128)} %stack_reshape_squeeze.39), channel_id=1, source_target_pairs={{0,1},{1,2},{2,3},{3,4},{4,5},{5,6},{6,7},{7,8},{8,9},{9,10},{10,1... | collective-permute-start | bytes 24584 | tf_op jit(solution)/shard_map/ppermute | solution.py:18
  223.2 51.0 %collective-permute-start.2 = (f32[1,2,1024]{2,1,0:T(2,128)}, f32[1,2,1024]{2,1,0:T(2,128)}, u32[]{:S(2)}, u32[]{:S(2)}) collective-permute-start(f32[1,2,1024]{2,1,0:T(2,128)} %stack_reshape_squeeze.38), channel_id=1, source_target_pairs={{1,0},{2,1},{3,2},{4,3},{5,4},{6,5},{7,6},{8,7},{9,8},{10,9},{11,1... | collective-permute-start | bytes 24584 | tf_op jit(solution)/shard_map/ppermute | solution.py:21
  359.8 19.8 %copy-start.34 = (f32[2,32,1024]{2,1,0:T(8,128)S(1)}, f32[2,32,1024]{2,1,0:T(8,128)}, u32[]{:S(2)}) copy-start(f32[2,32,1024]{2,1,0:T(8,128)} %copy-done.33) | copy-start | bytes 786436
  436.2 39.2 %collective-permute-start.5 = (f32[1,2,1024]{2,1,0:T(2,128)}, f32[1,2,1024]{2,1,0:T(2,128)}, u32[]{:S(2)}, u32[]{:S(2)}) collective-permute-start(f32[1,2,1024]{2,1,0:T(2,128)} %stack_reshape_squeeze.41), channel_id=1, source_target_pairs={{0,1},{1,2},{2,3},{3,4},{4,5},{5,6},{6,7},{7,8},{8,9},{9,10},{10,1... | collective-permute-start | bytes 24584 | tf_op jit(solution)/shard_map/ppermute | solution.py:18
  438.1 43.2 %collective-permute-start.4 = (f32[1,2,1024]{2,1,0:T(2,128)}, f32[1,2,1024]{2,1,0:T(2,128)}, u32[]{:S(2)}, u32[]{:S(2)}) collective-permute-start(f32[1,2,1024]{2,1,0:T(2,128)} %stack_reshape_squeeze.40), channel_id=1, source_target_pairs={{1,0},{2,1},{3,2},{4,3},{5,4},{6,5},{7,6},{8,7},{9,8},{10,9},{11,1... | collective-permute-start | bytes 24584 | tf_op jit(solution)/shard_map/ppermute | solution.py:21
  596.7 6.8 copy-start.8
  596.7 6.7 copy-start.151
  596.7 6.7 copy-start.153
  599.9 27.8 %collective-permute-start.7 = (f32[1,2,1024]{2,1,0:T(2,128)}, f32[1,2,1024]{2,1,0:T(2,128)}, u32[]{:S(2)}, u32[]{:S(2)}) collective-permute-start(f32[1,2,1024]{2,1,0:T(2,128)} %stack_reshape_squeeze.43), channel_id=1, source_target_pairs={{0,1},{1,2},{2,3},{3,4},{4,5},{5,6},{6,7},{7,8},{8,9},{9,10},{10,1... | collective-permute-start | bytes 24584 | tf_op jit(solution)/shard_map/ppermute | solution.py:18
  602.1 30.7 %collective-permute-start.6 = (f32[1,2,1024]{2,1,0:T(2,128)}, f32[1,2,1024]{2,1,0:T(2,128)}, u32[]{:S(2)}, u32[]{:S(2)}) collective-permute-start(f32[1,2,1024]{2,1,0:T(2,128)} %stack_reshape_squeeze.42), channel_id=1, source_target_pairs={{1,0},{2,1},{3,2},{4,3},{5,4},{6,5},{7,6},{8,7},{9,8},{10,9},{11,1... | collective-permute-start | bytes 24584 | tf_op jit(solution)/shard_map/ppermute | solution.py:21
  607.5 10.3 copy-start.22
  630.3 7.0 copy-start.12
  630.3 7.0 copy-start.14
  630.3 7.0 copy-start.16
  630.3 7.0 copy-start.18
  637.4 70.8 %copy-start.45 = (f32[2,32,1024]{2,1,0:T(8,128)S(1)}, f32[2,32,1024]{2,1,0:T(8,128)}, u32[]{:S(2)}) copy-start(f32[2,32,1024]{2,1,0:T(8,128)} %copy-done.44) | copy-start | bytes 786436
  709.7 18.3 %copy-start.54 = (f32[2,32,1024]{2,1,0:T(8,128)}, f32[2,32,1024]{2,1,0:T(8,128)S(1)}, u32[]{:S(2)}) copy-start(f32[2,32,1024]{2,1,0:T(8,128)S(1)} %get-tuple-element.47) | copy-start | bytes 786436
  783.5 36.6 %collective-permute-start.9 = (f32[1,2,1024]{2,1,0:T(2,128)}, f32[1,2,1024]{2,1,0:T(2,128)}, u32[]{:S(2)}, u32[]{:S(2)}) collective-permute-start(f32[1,2,1024]{2,1,0:T(2,128)} %stack_reshape_squeeze.45), channel_id=1, source_target_pairs={{0,1},{1,2},{2,3},{3,4},{4,5},{5,6},{6,7},{7,8},{8,9},{9,10},{10,1... | collective-permute-start | bytes 24584 | tf_op jit(solution)/shard_map/ppermute | solution.py:18
  785.4 40.6 %collective-permute-start.8 = (f32[1,2,1024]{2,1,0:T(2,128)}, f32[1,2,1024]{2,1,0:T(2,128)}, u32[]{:S(2)}, u32[]{:S(2)}) collective-permute-start(f32[1,2,1024]{2,1,0:T(2,128)} %stack_reshape_squeeze.44), channel_id=1, source_target_pairs={{1,0},{2,1},{3,2},{4,3},{5,4},{6,5},{7,6},{8,7},{9,8},{10,9},{11,1... | collective-permute-start | bytes 24584 | tf_op jit(solution)/shard_map/ppermute | solution.py:21
  823.6 8.3 copy-start.89
  823.6 8.3 copy-start.108
  823.6 8.3 copy-start.110
  823.6 8.3 copy-start.120
  913.2 19.4 %copy-start.36 = (f32[2,32,1024]{2,1,0:T(8,128)S(1)}, f32[2,32,1024]{2,1,0:T(8,128)}, u32[]{:S(2)}) copy-start(f32[2,32,1024]{2,1,0:T(8,128)} %copy-done.35) | copy-start | bytes 786436
  952.7 22.7 %collective-permute-start.11 = (f32[1,2,1024]{2,1,0:T(2,128)S(1)}, f32[1,2,1024]{2,1,0:T(2,128)S(1)}, u32[]{:S(2)}, u32[]{:S(2)}) collective-permute-start(f32[1,2,1024]{2,1,0:T(2,128)S(1)} %stack_reshape_squeeze.47), channel_id=1, source_target_pairs={{0,1},{1,2},{2,3},{3,4},{4,5},{5,6},{6,7},{7,8},{8,9},{9,10},{10,1... | collective-permute-start | bytes 24584 | tf_op jit(solution)/shard_map/ppermute | solution.py:18
  954.2 26.3 %collective-permute-start.10 = (f32[1,2,1024]{2,1,0:T(2,128)S(1)}, f32[1,2,1024]{2,1,0:T(2,128)S(1)}, u32[]{:S(2)}, u32[]{:S(2)}) collective-permute-start(f32[1,2,1024]{2,1,0:T(2,128)S(1)} %stack_reshape_squeeze.46), channel_id=1, source_target_pairs={{1,0},{2,1},{3,2},{4,3},{5,4},{6,5},{7,6},{8,7},{9,8},{10,9},{11,1... | collective-permute-start | bytes 24584 | tf_op jit(solution)/shard_map/ppermute | solution.py:21
  977.9 6.3 copy-start.15
  977.9 6.3 copy-start.17
  977.9 6.3 copy-start.19
  977.9 6.3 copy-start.50
  977.9 6.3 copy-start.53
  984.3 72.3 %copy-start.40 = (f32[1,1,2,32,1024]{4,3,2,1,0:T(8,128)S(1)}, f32[1,1,2,32,1024]{4,3,2,1,0:T(8,128)}, u32[]{:S(2)}) copy-start(f32[1,1,2,32,1024]{4,3,2,1,0:T(8,128)} %param.10) | copy-start | bytes 786436
  984.3 72.3 %copy-start.75 = (pred[32,1024]{1,0:T(8,128)(4,1)S(1)}, pred[32,1024]{1,0:T(8,128)(4,1)}, u32[]{:S(2)}) copy-start(pred[32,1024]{1,0:T(8,128)(4,1)} %copy-done.73) | copy-start | bytes 98308
  984.3 72.3 %copy-start.78 = (pred[32,1024]{1,0:T(8,128)(4,1)S(1)}, pred[32,1024]{1,0:T(8,128)(4,1)}, u32[]{:S(2)}) copy-start(pred[32,1024]{1,0:T(8,128)(4,1)} %copy-done.76) | copy-start | bytes 98308
  1056.6 6.0 copy-start.56
  (115 other events, 333.5 us)
where the time goes:
time: 1080 us; the launch traced here: 1060 us
  blocking collectives  547 us (51%)
  local copies, waits for them, and re-layouts  336 us (31%)
  other arithmetic  139 us (13%)
  starting transfers between devices  22.6 us (2%)
  between operations  15.9 us (1%)
    psum x5, blocking collectives, global_sum(): return lax.psum(jnp.sum(values), ('brick', 'grp'))  339 us
    another operation x3, blocking collectives, coarse_solve(): lax.linalg.triangular_solve(factor, gathered_terms, left_side=True, lower...  94.1 us
    all_gather x6, blocking collectives, apply_operator(): portion = lax.all_gather(outgoing_sides[None], 'brick', axis=0, tiled=True)  94.1 us
    broadcast_in_dim x26, local copies, waits for them, and re-layouts, apply_operator(): jnp.where(cube_third == BS - 1, from_above, jnp.roll(cube, -1, axis=3))  45 us
    broadcast_in_dim x26, local copies, waits for them, and re-layouts, apply_operator(): jnp.where(cube_third == 0, from_below, jnp.roll(cube, 1, axis=3))  43.7 us
    concatenate x12, local copies, waits for them, and re-layouts, apply_operator(): jnp.roll(cube, -1, axis=3)  26.6 us
    concatenate x12, local copies, waits for them, and re-layouts, apply_operator(): jnp.roll(cube, 1, axis=3)  25.4 us
    div x6, other arithmetic, precondition(): smoothed = OMEGA * residual_field / diagonal  24.1 us
  transfers between devices with their start and end apart: 12, of which 0 were waited for; matrix products, arithmetic and copies ran while one was open for 21% of the time, Pallas kernels for 0%

commit v1 on v0

--- a/solution.py
+++ b/solution.py
@@ -8,6 +8,16 @@
 PATCH_Y = 2
 ITERS = 3
 OMEGA = 0.6
+
+
+def turned_line(block, axis, d):
+    peers = lax.axis_size(axis)
+    moving, shards = (block, [block])
+    for _ in range(peers - 1):
+        moving = lax.ppermute(moving, axis, [(i, (i + 1) % peers) for i in range(peers)])
+        shards.insert(0, moving)
+    line = jnp.concatenate(shards, axis=d)
+    return jnp.roll(line, (lax.axis_index(axis) + 1) * block.shape[d], axis=d)
 
 
 def extended_2(block, sides, width):
@@ -119,7 +129,7 @@
                 pad_rows(grid_upper_y[:, PATCH_Y - 1], capacity),
             ]
         )
-        portion = lax.all_gather(outgoing_sides[None], "brick", axis=0, tiled=True)
+        portion = turned_line(outgoing_sides[None], "brick", 0)
         sources = jnp.arange(portion.shape[0], dtype=jnp.int32)
         matches = sources[:, None] == wanted[None, :]
         remote = jnp.zeros((4, capacity, face_size), jnp.float32) + jnp.sum(

time: 1080 us -> 1140 us (1.056)
  blocking collectives: 547 us -> 459 us
  starting transfers between devices: 22.6 us -> 85.1 us
  local copies, waits for them, and re-layouts: 336 us -> 374 us
  waiting for transfers between devices: 0.03 us -> 31.5 us
  other arithmetic: 139 us -> 155 us
    all_gather x6 -> x0, blocking collectives: 94.1 us -> none  [apply_operator(): portion = lax.all_gather(outgoing_sides[None], 'brick', axis=0, tiled=True)]
    ppermute x0 -> x42, starting transfers between devices: none -> 59.1 us  [turned_line(): lax.ppermute(moving, axis, [(i, (i + 1) % peers) for i in range(peers)])]
    ppermute x0 -> x42, waiting for transfers between devices: none -> 31.5 us  [turned_line(): lax.ppermute(moving, axis, [(i, (i + 1) % peers) for i in range(peers)])]
    unnamed x350 -> x326, local copies, waits for them, and re-layouts: 19.7 us -> 40 us
  transfers between devices with their start and end apart: 12 -> 54, of which waited for: 0 -> 19; matrix products, arithmetic and copies ran while one was open for 21% -> 28% of each run, Pallas kernels for 0% -> 0%
where the time goes in v1:
time: 1140 us; the launch traced here: 1120 us
  blocking collectives  459 us (40%)
  local copies, waits for them, and re-layouts  374 us (33%)
  other arithmetic  155 us (14%)
  starting transfers between devices  85.1 us (7%)
  waiting for transfers between devices  31.5 us (3%)
  between operations  15.5 us (1%)
    psum x5, blocking collectives, global_sum(): return lax.psum(jnp.sum(values), ('brick', 'grp'))  346 us
    another operation x3, blocking collectives, coarse_solve(): lax.linalg.triangular_solve(factor, gathered_terms, left_side=True, lower...  93.1 us
    ppermute x42, starting transfers between devices, turned_line(): lax.ppermute(moving, axis, [(i, (i + 1) % peers) for i in range(peers)])  59.1 us
    broadcast_in_dim x26, local copies, waits for them, and re-layouts, apply_operator(): jnp.where(cube_third == BS - 1, from_above, jnp.roll(cube, -1, axis=3))  44.4 us
    broadcast_in_dim x26, local copies, waits for them, and re-layouts, apply_operator(): jnp.where(cube_third == 0, from_below, jnp.roll(cube, 1, axis=3))  41 us
    unnamed x326, local copies, waits for them, and re-layouts  40 us
    ppermute x42, waiting for transfers between devices, turned_line(): lax.ppermute(moving, axis, [(i, (i + 1) % peers) for i in range(peers)])  31.5 us
    concatenate x12, local copies, waits for them, and re-layouts, apply_operator(): jnp.roll(cube, -1, axis=3)  26.6 us
  transfers between devices with their start and end apart: 54, of which 19 were waited for; matrix products, arithmetic and copies ran while one was open for 28% of the time, Pallas kernels for 0%

profile of v1, /device:TPU:1, one launch (start us, length us, event | category | flops | bytes accessed | tf_op | source)
XLA Modules:
  0.0 1123.8 jit_solution(7082862433695960275)
XLA Ops:
  5.9 2.6 multiply_divide_fusion.5
  10.8 2.7 collective-permute-start
  22.3 2.5 squeeze.120
  33.4 5.7 multiply_divide_fusion.2
  41.7 4.1 collective-permute-start.8
  57.4 19.9 %all-gather.4 = f32[16,4,2]{1,2,0:T(2,128)S(1)} all-gather(f32[1,4,2]{1,2,0:T(2,128)S(1)} %bitcast.576), channel_id=2, replica_groups=mesh['brick'=8,'grp'=16] {'grp'}, dimensions={0}, use_global_device_ids=true | all-gather | bytes 544 | tf_op jit(solution)/shard_map/all_gather | solution.py:199
  84.8 2.9 cholesky.19
  89.1 2.4 custom-call.14
  93.7 31.7 %all-reduce.18 = f32[32]{0:T(128)S(1)} all-reduce(f32[32]{0:T(128)S(1)} %dynamic-update-slice.3), channel_id=3, replica_groups=mesh['brick'=8,'grp'=16] {'grp'}, use_global_device_ids=true, to_apply=%add.18 | all-reduce | flops 32 | bytes 256 | tf_op jit(solution)/shard_map/triangular_solve/reshape.87 | solution.py:207
  125.4 12.7 %collective-permute-start.1 = (f32[1,4,2,1024]{3,1,2,0:T(4,128)}, f32[1,4,2,1024]{3,1,2,0:T(4,128)S(1)}, u32[]{:S(2)}, u32[]{:S(2)}) collective-permute-start(f32[1,4,2,1024]{3,1,2,0:T(4,128)} %collective-permute-done), channel_id=1, source_target_pairs={{0,16},{16,32},{32,48},{48,64},{64,80},{80,96},{96,112},{112,0},{1... | collective-permute-start | bytes 98312 | tf_op jit(solution)/shard_map/ppermute | solution.py:17
  149.0 2.5 collective-permute-done.4
  152.9 3.4 collective-permute-done.5
  185.3 8.4 fusion.46
  193.8 2.4 concatenate.665
  210.3 2.4 broadcast_in_dim.743
  212.7 2.4 broadcast_in_dim.745
  225.5 3.6 collective-permute-done.12
  236.4 3.0 pad_maximum_fusion.2
  245.4 2.4 concatenate.699
  250.3 2.4 concatenate.751
  276.3 2.4 broadcast_in_dim.761
  278.7 2.4 broadcast_in_dim.726
  298.2 3.7 multiply_reduce_fusion.3
  301.9 68.6 %all-reduce.21 = (f32[]{:T(128)}, f32[]{:T(128)}) all-reduce(f32[]{:T(128)} %get-tuple-element.18, f32[]{:T(128)} %get-tuple-element.17), channel_id=1, replica_groups=mesh['brick'=8,'grp'=16] {'brick','grp'}, use_global_device_ids=true, to_apply=%region_16.20 | all-reduce | flops 2 | bytes 16 | tf_op jit(solution)/shard_map/psum | solution.py:223
  382.4 8.8 multiply_divide_fusion.1
  406.3 2.7 collective-permute-start.26
  409.0 4.1 fusion.108
  417.0 30.0 %all-reduce.19 = f32[32]{0:T(128)} all-reduce(f32[32]{0:T(128)} %dynamic-update-slice.4), channel_id=4, replica_groups=mesh['brick'=8,'grp'=16] {'grp'}, use_global_device_ids=true, to_apply=%add.19 | all-reduce | flops 32 | bytes 256 | tf_op jit(solution)/shard_map/triangular_solve/reshape.87 | solution.py:207
  447.0 7.7 collective-permute-start.20
  462.0 3.1 pad_maximum_fusion.4
  471.1 2.4 concatenate.765
  475.9 2.4 concatenate.766
  478.4 2.4 concatenate.719
  491.2 2.4 broadcast_in_dim.752
  499.5 2.4 broadcast_in_dim.749
  516.2 3.7 multiply_reduce_fusion.2
  519.9 68.0 %psum.44 = f32[]{:T(128)} all-reduce(f32[]{:T(128)} %get-tuple-element.61), channel_id=1, replica_groups=mesh['brick'=8,'grp'=16] {'brick','grp'}, use_global_device_ids=true, to_apply=%region_23.27 | all-reduce | flops 1 | bytes 8 | tf_op jit(solution)/shard_map/psum | solution.py:223
  603.2 7.3 multiply_add_fusion.1
  618.6 2.6 collective-permute-done.30
  625.0 3.6 collective-permute-start.35
  630.7 2.7 pad_maximum_fusion.6
  641.8 2.5 concatenate.818
  655.4 2.5 broadcast_in_dim.780
  657.9 2.4 broadcast_in_dim.757
  671.5 3.4 multiply_reduce_fusion.1
  674.9 70.2 %psum.45 = f32[]{:T(128)} all-reduce(f32[]{:T(128)} %get-tuple-element.57), channel_id=1, replica_groups=mesh['brick'=8,'grp'=16] {'brick','grp'}, use_global_device_ids=true, to_apply=%region_26.30 | all-reduce | flops 1 | bytes 8 | tf_op jit(solution)/shard_map/psum | solution.py:223
  757.1 8.1 multiply_divide_fusion
  784.4 31.4 %all-reduce.20 = f32[32]{0:T(128)} all-reduce(f32[32]{0:T(128)} %dynamic-update-slice.5), channel_id=5, replica_groups=mesh['brick'=8,'grp'=16] {'grp'}, use_global_device_ids=true, to_apply=%add.20 | all-reduce | flops 32 | bytes 256 | tf_op jit(solution)/shard_map/triangular_solve/reshape.87 | solution.py:207
  815.8 7.2 collective-permute-start.38
  833.7 3.0 pad_maximum_fusion.8
  845.8 2.4 concatenate.783
  861.0 2.4 broadcast_in_dim.783
  869.3 2.4 broadcast_in_dim.782
  871.7 2.4 broadcast_in_dim.768
  888.5 3.9 multiply_reduce_fusion
  892.4 68.5 %psum.46 = f32[]{:T(128)} all-reduce(f32[]{:T(128)} %get-tuple-element.49), channel_id=1, replica_groups=mesh['brick'=8,'grp'=16] {'brick','grp'}, use_global_device_ids=true, to_apply=%region_30.34 | all-reduce | flops 1 | bytes 8 | tf_op jit(solution)/shard_map/psum | solution.py:223
  981.7 10.7 multiply_add_fusion
  1003.9 2.8 collective-permute-start.53
  1010.4 3.1 collective-permute-done.50
  1027.8 2.5 broadcast_in_dim.784
  1030.3 2.4 broadcast_in_dim.776
  1041.3 2.6 fusion.173
  1044.7 70.2 %psum.47 = f32[]{:T(128)} all-reduce(f32[]{:T(128)} %fusion.173), channel_id=1, replica_groups=mesh['brick'=8,'grp'=16] {'brick','grp'}, use_global_device_ids=true, to_apply=%region_33.37 | all-reduce | flops 1 | bytes 8 | tf_op jit(solution)/shard_map/psum | solution.py:223
  1116.4 6.0 fusion.161
  (750 shorter events, 441.0 us)
Async XLA Ops:
  4.5 28.9 %copy-start.75 = (pred[32]{0:T(512)(128)(4,1)}, pred[32]{0:T(512)(128)(4,1)S(1)}, u32[]{:S(2)}) copy-start(pred[32]{0:T(512)(128)(4,1)S(1)} %get-tuple-element.276) | copy-start | bytes 100
  4.5 28.9 %copy-start.79 = (pred[32]{0:T(512)(128)(4,1)}, pred[32]{0:T(512)(128)(4,1)S(1)}, u32[]{:S(2)}) copy-start(pred[32]{0:T(512)(128)(4,1)S(1)} %get-tuple-element.277) | copy-start | bytes 100
  5.7 83.3 %copy-start.70 = (f32[2]{0:T(128)}, f32[2]{0:T(128)S(1)}, u32[]{:S(2)}) copy-start(f32[2]{0:T(128)S(1)} %get-tuple-element.39) | copy-start | bytes 28
  8.6 47.9 %copy-start.13 = (f32[2,32,1024]{2,1,0:T(8,128)}, f32[2,32,1024]{2,1,0:T(8,128)S(1)}, u32[]{:S(2)}) copy-start(f32[2,32,1024]{2,1,0:T(8,128)S(1)} %get-tuple-element.80) | copy-start | bytes 786436
  8.6 507.6 %copy-start.11 = (f32[2,32,1024]{2,1,0:T(8,128)}, f32[2,32,1024]{2,1,0:T(8,128)S(1)}, u32[]{:S(2)}) copy-start(f32[2,32,1024]{2,1,0:T(8,128)S(1)} %get-tuple-element.79) | copy-start | bytes 786436
  10.8 114.6 %collective-permute-start = (f32[1,4,2,1024]{3,1,2,0:T(4,128)}, f32[1,4,2,1024]{3,1,2,0:T(4,128)}, u32[]{:S(2)}, u32[]{:S(2)}) collective-permute-start(f32[1,4,2,1024]{3,1,2,0:T(4,128)} %maximum_bitcast_fusion), channel_id=1, source_target_pairs={{0,16},{16,32},{32,48},{48,64},{64,80},{80,96},{96,112},{112,0},{1... | collective-permute-start | bytes 98312 | tf_op jit(solution)/shard_map/ppermute | solution.py:17
  41.7 123.7 %collective-permute-start.8 = (f32[1,2,1024]{2,1,0:T(2,128)}, f32[1,2,1024]{2,1,0:T(2,128)}, u32[]{:S(2)}, u32[]{:S(2)}) collective-permute-start(f32[1,2,1024]{2,1,0:T(2,128)} %stack_reshape_squeeze.37), channel_id=1, source_target_pairs={{0,1},{1,2},{2,3},{3,4},{4,5},{5,6},{6,7},{7,8},{8,9},{9,10},{10,1... | collective-permute-start | bytes 24584 | tf_op jit(solution)/shard_map/ppermute | solution.py:28
  46.5 116.6 %collective-permute-start.7 = (f32[1,2,1024]{2,1,0:T(2,128)}, f32[1,2,1024]{2,1,0:T(2,128)}, u32[]{:S(2)}, u32[]{:S(2)}) collective-permute-start(f32[1,2,1024]{2,1,0:T(2,128)} %stack_reshape_squeeze.36), channel_id=1, source_target_pairs={{1,0},{2,1},{3,2},{4,3},{5,4},{6,5},{7,6},{8,7},{9,8},{10,9},{11,1... | collective-permute-start | bytes 24584 | tf_op jit(solution)/shard_map/ppermute | solution.py:31
  80.5 81.3 %copy-start.54 = (f32[2,31,1024]{2,1,0:T(8,128)S(1)}, f32[2,31,1024]{2,1,0:T(8,128)}, u32[]{:S(2)}) copy-start(f32[2,31,1024]{2,1,0:T(8,128)} %get-tuple-element.150) | copy-start | bytes 761860
  125.4 14.1 %collective-permute-start.1 = (f32[1,4,2,1024]{3,1,2,0:T(4,128)}, f32[1,4,2,1024]{3,1,2,0:T(4,128)S(1)}, u32[]{:S(2)}, u32[]{:S(2)}) collective-permute-start(f32[1,4,2,1024]{3,1,2,0:T(4,128)} %collective-permute-done), channel_id=1, source_target_pairs={{0,16},{16,32},{32,48},{48,64},{64,80},{80,96},{96,112},{112,0},{1... | collective-permute-start | bytes 98312 | tf_op jit(solution)/shard_map/ppermute | solution.py:17
  139.5 3.2 collective-permute-start.2
  142.7 6.2 collective-permute-start.3
  148.9 2.6 collective-permute-start.4
  151.6 4.7 collective-permute-start.5
  156.2 15.2 %collective-permute-start.6 = (f32[1,4,2,1024]{3,1,2,0:T(4,128)}, f32[1,4,2,1024]{3,1,2,0:T(4,128)}, u32[]{:S(2)}, u32[]{:S(2)}) collective-permute-start(f32[1,4,2,1024]{3,1,2,0:T(4,128)} %collective-permute-done.5), channel_id=1, source_target_pairs={{0,16},{16,32},{32,48},{48,64},{64,80},{80,96},{96,112},{112,0},{1... | collective-permute-start | bytes 98312 | tf_op jit(solution)/shard_map/ppermute | solution.py:17
  210.3 4.9 collective-permute-start.9
  215.2 4.7 collective-permute-start.10
  219.9 4.6 collective-permute-start.11
  224.5 4.7 collective-permute-start.12
  229.1 7.3 collective-permute-start.13
  233.1 31.4 %collective-permute-start.17 = (f32[1,2,1024]{2,1,0:T(2,128)}, f32[1,2,1024]{2,1,0:T(2,128)}, u32[]{:S(2)}, u32[]{:S(2)}) collective-permute-start(f32[1,2,1024]{2,1,0:T(2,128)} %stack_reshape_squeeze.39), channel_id=1, source_target_pairs={{0,1},{1,2},{2,3},{3,4},{4,5},{5,6},{6,7},{7,8},{8,9},{9,10},{10,1... | collective-permute-start | bytes 24584 | tf_op jit(solution)/shard_map/ppermute | solution.py:28
  234.9 37.9 %collective-permute-start.16 = (f32[1,2,1024]{2,1,0:T(2,128)}, f32[1,2,1024]{2,1,0:T(2,128)}, u32[]{:S(2)}, u32[]{:S(2)}) collective-permute-start(f32[1,2,1024]{2,1,0:T(2,128)} %stack_reshape_squeeze.38), channel_id=1, source_target_pairs={{1,0},{2,1},{3,2},{4,3},{5,4},{6,5},{7,6},{8,7},{9,8},{10,9},{11,1... | collective-permute-start | bytes 24584 | tf_op jit(solution)/shard_map/ppermute | solution.py:31
  236.4 4.9 collective-permute-start.14
  241.3 39.8 %collective-permute-start.15 = (f32[1,4,2,1024]{3,1,2,0:T(4,128)}, f32[1,4,2,1024]{3,1,2,0:T(4,128)}, u32[]{:S(2)}, u32[]{:S(2)}) collective-permute-start(f32[1,4,2,1024]{3,1,2,0:T(4,128)} %collective-permute-done.14), channel_id=1, source_target_pairs={{0,16},{16,32},{32,48},{48,64},{64,80},{80,96},{96,112},{112,0},{1... | collective-permute-start | bytes 98312 | tf_op jit(solution)/shard_map/ppermute | solution.py:17
  403.2 11.0 collective-permute-start.18
  406.3 79.0 %collective-permute-start.26 = (f32[1,2,1024]{2,1,0:T(2,128)}, f32[1,2,1024]{2,1,0:T(2,128)}, u32[]{:S(2)}, u32[]{:S(2)}) collective-permute-start(f32[1,2,1024]{2,1,0:T(2,128)} %stack_reshape_squeeze.41), channel_id=1, source_target_pairs={{0,1},{1,2},{2,3},{3,4},{4,5},{5,6},{6,7},{7,8},{8,9},{9,10},{10,1... | collective-permute-start | bytes 24584 | tf_op jit(solution)/shard_map/ppermute | solution.py:28
  414.2 32.8 %collective-permute-start.19 = (f32[1,4,2,1024]{3,1,2,0:T(4,128)}, f32[1,4,2,1024]{3,1,2,0:T(4,128)}, u32[]{:S(2)}, u32[]{:S(2)}) collective-permute-start(f32[1,4,2,1024]{3,1,2,0:T(4,128)} %collective-permute-done.18), channel_id=1, source_target_pairs={{0,16},{16,32},{32,48},{48,64},{64,80},{80,96},{96,112},{112,0},{1... | collective-permute-start | bytes 98312 | tf_op jit(solution)/shard_map/ppermute | solution.py:17
  447.0 9.0 collective-permute-start.20
  456.0 5.9 collective-permute-start.21
  460.4 33.2 %collective-permute-start.25 = (f32[1,2,1024]{2,1,0:T(2,128)}, f32[1,2,1024]{2,1,0:T(2,128)}, u32[]{:S(2)}, u32[]{:S(2)}) collective-permute-start(f32[1,2,1024]{2,1,0:T(2,128)} %stack_reshape_squeeze.40), channel_id=1, source_target_pairs={{1,0},{2,1},{3,2},{4,3},{5,4},{6,5},{7,6},{8,7},{9,8},{10,9},{11,1... | collective-permute-start | bytes 24584 | tf_op jit(solution)/shard_map/ppermute | solution.py:31
  462.0 3.2 collective-permute-start.22
  465.2 4.7 collective-permute-start.23
  469.9 32.1 %collective-permute-start.24 = (f32[1,4,2,1024]{3,1,2,0:T(4,128)}, f32[1,4,2,1024]{3,1,2,0:T(4,128)}, u32[]{:S(2)}, u32[]{:S(2)}) collective-permute-start(f32[1,4,2,1024]{3,1,2,0:T(4,128)} %collective-permute-done.23), channel_id=1, source_target_pairs={{0,16},{16,32},{32,48},{48,64},{64,80},{80,96},{96,112},{112,0},{1... | collective-permute-start | bytes 98312 | tf_op jit(solution)/shard_map/ppermute | solution.py:17
  598.1 12.5 %collective-permute-start.27 = (f32[1,4,2,1024]{3,1,2,0:T(4,128)}, f32[1,4,2,1024]{3,1,2,0:T(4,128)}, u32[]{:S(2)}, u32[]{:S(2)}) collective-permute-start(f32[1,4,2,1024]{3,1,2,0:T(4,128)} %maximum_bitcast_fusion.3), channel_id=1, source_target_pairs={{0,16},{16,32},{32,48},{48,64},{64,80},{80,96},{96,112},{112,0},{1... | collective-permute-start | bytes 98312 | tf_op jit(solution)/shard_map/ppermute | solution.py:17
  610.5 1.4 collective-permute-start.28
  612.0 4.5 collective-permute-start.29
  616.5 4.7 collective-permute-start.30
  621.2 9.2 collective-permute-start.31
  625.0 24.1 %collective-permute-start.35 = (f32[1,2,1024]{2,1,0:T(2,128)}, f32[1,2,1024]{2,1,0:T(2,128)}, u32[]{:S(2)}, u32[]{:S(2)}) collective-permute-start(f32[1,2,1024]{2,1,0:T(2,128)} %stack_reshape_squeeze.43), channel_id=1, source_target_pairs={{0,1},{1,2},{2,3},{3,4},{4,5},{5,6},{6,7},{7,8},{8,9},{9,10},{10,1... | collective-permute-start | bytes 24584 | tf_op jit(solution)/shard_map/ppermute | solution.py:28
  628.6 24.0 %collective-permute-start.34 = (f32[1,2,1024]{2,1,0:T(2,128)}, f32[1,2,1024]{2,1,0:T(2,128)}, u32[]{:S(2)}, u32[]{:S(2)}) collective-permute-start(f32[1,2,1024]{2,1,0:T(2,128)} %stack_reshape_squeeze.42), channel_id=1, source_target_pairs={{1,0},{2,1},{3,2},{4,3},{5,4},{6,5},{7,6},{8,7},{9,8},{10,9},{11,1... | collective-permute-start | bytes 24584 | tf_op jit(solution)/shard_map/ppermute | solution.py:31
  630.4 4.9 collective-permute-start.32
  635.3 25.0 %collective-permute-start.33 = (f32[1,4,2,1024]{3,1,2,0:T(4,128)}, f32[1,4,2,1024]{3,1,2,0:T(4,128)}, u32[]{:S(2)}, u32[]{:S(2)}) collective-permute-start(f32[1,4,2,1024]{3,1,2,0:T(4,128)} %collective-permute-done.32), channel_id=1, source_target_pairs={{0,16},{16,32},{32,48},{48,64},{64,80},{80,96},{96,112},{112,0},{1... | collective-permute-start | bytes 98312 | tf_op jit(solution)/shard_map/ppermute | solution.py:17
  671.5 75.0 %copy-start.44 = (f32[2,32,1024]{2,1,0:T(8,128)S(1)}, f32[2,32,1024]{2,1,0:T(8,128)}, u32[]{:S(2)}) copy-start(f32[2,32,1024]{2,1,0:T(8,128)} %copy-done.43) | copy-start | bytes 786436
  776.8 3.3 collective-permute-start.36
  780.1 35.7 %collective-permute-start.37 = (f32[1,4,2,1024]{3,1,2,0:T(4,128)}, f32[1,4,2,1024]{3,1,2,0:T(4,128)}, u32[]{:S(2)}, u32[]{:S(2)}) collective-permute-start(f32[1,4,2,1024]{3,1,2,0:T(4,128)} %collective-permute-done.36), channel_id=1, source_target_pairs={{0,16},{16,32},{32,48},{48,64},{64,80},{80,96},{96,112},{112,0},{1... | collective-permute-start | bytes 98312 | tf_op jit(solution)/shard_map/ppermute | solution.py:17
  815.8 9.1 collective-permute-start.38
  824.9 8.8 collective-permute-start.39
  830.3 27.3 %collective-permute-start.44 = (f32[1,2,1024]{2,1,0:T(2,128)}, f32[1,2,1024]{2,1,0:T(2,128)}, u32[]{:S(2)}, u32[]{:S(2)}) collective-permute-start(f32[1,2,1024]{2,1,0:T(2,128)} %stack_reshape_squeeze.45), channel_id=1, source_target_pairs={{0,1},{1,2},{2,3},{3,4},{4,5},{5,6},{6,7},{7,8},{8,9},{9,10},{10,1... | collective-permute-start | bytes 24584 | tf_op jit(solution)/shard_map/ppermute | solution.py:28
  832.2 33.7 %collective-permute-start.43 = (f32[1,2,1024]{2,1,0:T(2,128)}, f32[1,2,1024]{2,1,0:T(2,128)}, u32[]{:S(2)}, u32[]{:S(2)}) collective-permute-start(f32[1,2,1024]{2,1,0:T(2,128)} %stack_reshape_squeeze.44), channel_id=1, source_target_pairs={{1,0},{2,1},{3,2},{4,3},{5,4},{6,5},{7,6},{8,7},{9,8},{10,9},{11,1... | collective-permute-start | bytes 24584 | tf_op jit(solution)/shard_map/ppermute | solution.py:31
  833.7 3.0 collective-permute-start.40
  836.7 4.6 collective-permute-start.41
  841.3 32.9 %collective-permute-start.42 = (f32[1,4,2,1024]{3,1,2,0:T(4,128)}, f32[1,4,2,1024]{3,1,2,0:T(4,128)}, u32[]{:S(2)}, u32[]{:S(2)}) collective-permute-start(f32[1,4,2,1024]{3,1,2,0:T(4,128)} %collective-permute-done.41), channel_id=1, source_target_pairs={{0,16},{16,32},{32,48},{48,64},{64,80},{80,96},{96,112},{112,0},{1... | collective-permute-start | bytes 98312 | tf_op jit(solution)/shard_map/ppermute | solution.py:17
  975.5 17.0 %collective-permute-start.45 = (f32[1,4,2,1024]{3,1,2,0:T(4,128)}, f32[1,4,2,1024]{3,1,2,0:T(4,128)}, u32[]{:S(2)}, u32[]{:S(2)}) collective-permute-start(f32[1,4,2,1024]{3,1,2,0:T(4,128)} %maximum_bitcast_fusion.5), channel_id=1, source_target_pairs={{0,16},{16,32},{32,48},{48,64},{64,80},{80,96},{96,112},{112,0},{1... | collective-permute-start | bytes 98312 | tf_op jit(solution)/shard_map/ppermute | solution.py:17
  992.4 1.7 collective-permute-start.46
  994.2 3.7 collective-permute-start.47
  997.9 3.5 collective-permute-start.48
  1001.5 6.8 collective-permute-start.49
  1003.9 19.6 %collective-permute-start.53 = (f32[1,2,1024]{2,1,0:T(2,128)S(1)}, f32[1,2,1024]{2,1,0:T(2,128)S(1)}, u32[]{:S(2)}, u32[]{:S(2)}) collective-permute-start(f32[1,2,1024]{2,1,0:T(2,128)S(1)} %stack_reshape_squeeze.47), channel_id=1, source_target_pairs={{0,1},{1,2},{2,3},{3,4},{4,5},{5,6},{6,7},{7,8},{8,9},{9,10},{10,1... | collective-permute-start | bytes 24584 | tf_op jit(solution)/shard_map/ppermute | solution.py:28
  1006.7 19.6 %collective-permute-start.52 = (f32[1,2,1024]{2,1,0:T(2,128)S(1)}, f32[1,2,1024]{2,1,0:T(2,128)S(1)}, u32[]{:S(2)}, u32[]{:S(2)}) collective-permute-start(f32[1,2,1024]{2,1,0:T(2,128)S(1)} %stack_reshape_squeeze.46), channel_id=1, source_target_pairs={{1,0},{2,1},{3,2},{4,3},{5,4},{6,5},{7,6},{8,7},{9,8},{10,9},{11,1... | collective-permute-start | bytes 24584 | tf_op jit(solution)/shard_map/ppermute | solution.py:31
  1008.3 5.2 collective-permute-start.50
  1013.5 19.2 %collective-permute-start.51 = (f32[1,4,2,1024]{3,1,2,0:T(4,128)}, f32[1,4,2,1024]{3,1,2,0:T(4,128)}, u32[]{:S(2)}, u32[]{:S(2)}) collective-permute-start(f32[1,4,2,1024]{3,1,2,0:T(4,128)} %collective-permute-done.50), channel_id=1, source_target_pairs={{0,16},{16,32},{32,48},{48,64},{64,80},{80,96},{96,112},{112,0},{1... | collective-permute-start | bytes 98312 | tf_op jit(solution)/shard_map/ppermute | solution.py:17
  1041.3 75.0 %copy-start.39 = (f32[1,1,2,32,1024]{4,3,2,1,0:T(8,128)S(1)}, f32[1,1,2,32,1024]{4,3,2,1,0:T(8,128)}, u32[]{:S(2)}) copy-start(f32[1,1,2,32,1024]{4,3,2,1,0:T(8,128)} %param.12) | copy-start | bytes 786436
  1041.3 75.0 %copy-start.58 = (pred[32,1024]{1,0:T(8,128)(4,1)S(1)}, pred[32,1024]{1,0:T(8,128)(4,1)}, u32[]{:S(2)}) copy-start(pred[32,1024]{1,0:T(8,128)(4,1)} %copy-done.57) | copy-start | bytes 98308
  1041.3 75.0 %copy-start.60 = (pred[32,1024]{1,0:T(8,128)(4,1)S(1)}, pred[32,1024]{1,0:T(8,128)(4,1)}, u32[]{:S(2)}) copy-start(pred[32,1024]{1,0:T(8,128)(4,1)} %copy-done.59) | copy-start | bytes 98308
  (130 other events, 1006.9 us)
